TPU v7x, 32 devices: a whole 2x2x4 slice. The times are simulated.
32 devices in a mesh: row: 2 (over y), col: 16 (over z, x, core).
Axes of the slice: x: 2, y: 2, z: 4, core: 2. Of those that a mesh axis runs over, the one named last changes fastest.
Arguments:
- velocity: bfloat16 [3, 512, 1024, 256], P(None, 'row', 'col'), may hold values from -6 to 6
- adj_temp: bfloat16 [512, 1024, 256], P('row', 'col'), may hold values from -6 to 6
- radial_div: bfloat16 [256, 256], replicated, may hold values from -0.375 to 0.375
- reciprocal_distance: float32 [256], replicated, may hold values from 0.002 to 0.02
- radial_basis: bfloat16 [168, 256, 256], P('row'), may hold values from -0.375 to 0.375
- radial_eig: float32 [168, 256], P('row'), may hold values from 0.5 to 8
- axial_diff: bfloat16 [1024, 1024], replicated, may hold values from -0.1875 to 0.1875
- axial_basis: bfloat16 [1024, 1024], replicated, may hold values from -0.1875 to 0.1875
- axial_eig: float32 [1024], replicated, may hold values from 0.5 to 8
Outputs:
- new_temp: float32 [168, 2, 1024, 256], P('row', None, 'col')
All inputs are finite; a program needn't handle non-finite values.
Results may differ from a plain program's by a relative error of at most 0.0055.
Values may be sent and summed in bfloat16 or wider, within the bound.
A program may use at most 256 MiB of HBM per device.

v0:
```python
import math

import jax
import jax.numpy as jnp
from jax import lax
from jax.sharding import PartitionSpec as P

HEAT_OFFSET = 1.0


def azimuth_table(mode_count, angle_count, circle):
    mode_ids = jnp.arange(mode_count, dtype=jnp.int32)
    angle_ids = jnp.arange(angle_count, dtype=jnp.int32)
    phase_index = mode_ids[:, None] * angle_ids[None, :] % circle
    angle_value = phase_index.astype(jnp.float32) * (2.0 * math.pi / circle)
    norm_factor = 1.0 / math.sqrt(circle)
    wave_table = jnp.stack(
        [jnp.cos(angle_value) * norm_factor, -jnp.sin(angle_value) * norm_factor], axis=1
    )
    return wave_table.astype(jnp.bfloat16).reshape(mode_count * 2, angle_count)


def body(
    velocity,
    adj_temp,
    radial_div,
    reciprocal_distance,
    radial_basis,
    radial_eig,
    axial_diff,
    axial_basis,
    axial_eig,
):
    highest = lax.Precision.HIGHEST
    fluxes = (velocity.astype(jnp.float32) * adj_temp.astype(jnp.float32)[None]).astype(
        jnp.bfloat16
    )
    fields = jnp.concatenate([fluxes, adj_temp[None]], axis=0)
    row_total = lax.axis_size("row")
    col_total = lax.axis_size("col")
    row_place = lax.axis_index("row")
    col_place = lax.axis_index("col")
    mode_rows = radial_basis.shape[0]
    angle_rows = fields.shape[1]
    radial_points = fields.shape[3]
    own_axial = fields.shape[2]
    circle = angle_rows * row_total
    azimuth_rows = lax.all_to_all(fields, "row", split_axis=2, concat_axis=1, tiled=True)
    wave_table = azimuth_table(mode_rows * row_total, circle, circle)
    spectra = jnp.einsum(
        "qt,ftzr->fqzr", wave_table, azimuth_rows, preferred_element_type=jnp.float32
    ).astype(jnp.bfloat16)
    spectra = spectra.reshape(4, mode_rows * row_total, 2, azimuth_rows.shape[2], radial_points)
    spectra = lax.all_to_all(spectra, "row", split_axis=1, concat_axis=3, tiled=True)
    radial_flux = spectra[0]
    angular_flux = spectra[1]
    axial_flux = spectra[2]
    thermal_state = spectra[3]
    mode_values = (row_place * mode_rows + jnp.arange(mode_rows, dtype=jnp.int32)).astype(
        jnp.float32
    )
    cylinder_aggregate = jnp.einsum(
        "mpzj,rj->mpzr", radial_flux, radial_div, preferred_element_type=jnp.float32
    )
    eigenbasis_projection = jnp.stack([-angular_flux[:, 1], angular_flux[:, 0]], axis=1).astype(
        jnp.float32
    )
    forcing_contribution = (
        HEAT_OFFSET * thermal_state.astype(jnp.float32)
        + cylinder_aggregate
        + mode_values[:, None, None, None] * reciprocal_distance * eigenbasis_projection
    )
    forcing_contribution = forcing_contribution.astype(jnp.bfloat16)
    own_count = radial_points // col_total
    source_hat = jnp.einsum(
        "mpzr,mri->mpiz", forcing_contribution, radial_basis, preferred_element_type=jnp.float32
    )
    flux_hat = jnp.einsum(
        "mpzr,mri->mpiz", axial_flux, radial_basis, preferred_element_type=jnp.float32
    )
    source_hat = source_hat.reshape(mode_rows, 2, col_total, own_count * own_axial)
    flux_hat = flux_hat.reshape(mode_rows, 2, col_total, own_count * own_axial)
    source_lines, flux_lines = (
        lax.all_to_all(source_hat, "col", split_axis=2, concat_axis=2, tiled=True),
        lax.all_to_all(flux_hat, "col", split_axis=2, concat_axis=2, tiled=True),
    )
    source_lines = source_lines.reshape(mode_rows, 2, col_total, own_count, own_axial)
    flux_lines = flux_lines.reshape(mode_rows, 2, col_total, own_count, own_axial)
    axial_points = axial_basis.shape[0]
    axial_vectors = axial_basis.astype(jnp.float32)
    axial_blocks = axial_vectors.reshape(col_total, own_axial, axial_points)
    axial_matrix = axial_diff.astype(jnp.float32)
    coefficients = jnp.einsum("mpsxy,syk->mpxk", source_lines, axial_blocks, precision=highest)
    derived_flux = jnp.einsum(
        "mpsxy,zsy->mpxz",
        flux_lines,
        axial_matrix.reshape(axial_points, col_total, own_axial),
        precision=highest,
    )
    coefficients = coefficients + jnp.einsum(
        "mpxz,zk->mpxk", derived_flux, axial_vectors, precision=highest
    )
    radial_values = lax.dynamic_slice_in_dim(radial_eig, col_place * own_count, own_count, 1)
    coefficients = coefficients / (radial_values[:, None, :, None] + axial_eig + HEAT_OFFSET)
    returned = jnp.einsum("mpxk,syk->mpsxy", coefficients, axial_blocks, precision=highest)
    returned = returned.reshape(mode_rows, 2, col_total, own_count * own_axial)
    returned = lax.all_to_all(returned, "col", split_axis=2, concat_axis=2, tiled=True)
    returned = returned.reshape(mode_rows, 2, col_total, own_count, own_axial)
    radial_vectors = radial_basis.astype(jnp.float32).reshape(
        mode_rows, radial_points, col_total, own_count
    )
    return jnp.einsum("mpsxy,mrsx->mpyr", returned, radial_vectors, precision=highest)


def solution(mesh):
    in_specs = (
        P(None, "row", "col", None),
        P("row", "col", None),
        P(),
        P(),
        P("row", None, None),
        P("row", None),
        P(),
        P(),
        P(),
    )
    out_specs = P("row", None, "col", None)
    return jax.shard_map(body, mesh=mesh, in_specs=in_specs, out_specs=out_specs, check_vma=False)
```

profile of v0, /device:TPU:11, one launch (start us, length us, event | category | flops | bytes accessed | tf_op | source)
XLA Modules:
  0.0 1895.7 jit_solution(12921515199878527278)
XLA Ops:
  25.7 23.2 %multiply_convert_fusion = bf16[3,256,64,256]{3,1,0,2:T(8,128)(2,1)} fusion(bf16[3,256,64,256]{3,2,1,0:T(8,128)(2,1)} %param.9, f32[256,64,256]{2,0,1:T(8,128)} %copy.62), kind=kLoop, calls=%fused_computation | loop fusion | flops 37748736 | bytes 67108864 | tf_op jit(solution)/shard_map/convert_element_type | solution.py:35
  48.9 23.0 %pad_maximum_fusion = bf16[4,256,64,256]{3,1,0,2:T(8,128)(2,1)} fusion(bf16[1,256,64,256]{3,1,0,2:T(8,128)(2,1)} %bitcast.129, bf16[3,256,64,256]{3,1,0,2:T(8,128)(2,1)} %multiply_convert_fusion), kind=kLoop, calls=%fused_computation.1 | loop fusion | flops 16777216 | bytes 67108864 | tf_op jit(solution)/shard_map/concatenate | solution.py:38
  87.0 359.5 %all-to-all-done = bf16[4,256,64,256]{3,1,0,2:T(8,128)(2,1)} async-done(((bf16[4,256,64,256]{3,1,0,2:T(8,128)(2,1)}), bf16[4,256,64,256]{3,1,0,2:T(8,128)(2,1)}, u32[]{:S(2)}, u32[]{:S(2)}) %all-to-all-start) | async-done | bytes 33554464 | tf_op jit(solution)/shard_map/all_to_all | solution.py:48
  446.5 23.0 %copy.64 = bf16[4,256,2,32,256]{4,1,2,3,0:T(8,128)(2,1)} copy(bf16[4,256,2,32,256]{4,1,0,3,2:T(8,128)(2,1)} %bitcast.1) | data formatting | bytes 67108864 | tf_op jit(solution)/shard_map/all_to_all | solution.py:48
  469.5 27.1 %convert_bitcast_fusion = bf16[4,336,32,256]{3,1,2,0:T(8,128)(2,1)} fusion(bf16[4,512,32,256]{3,1,2,0:T(8,128)(2,1)} %bitcast.128, bf16[336,512,1,1]{1,0,2,3:T(8,128)(2,1)S(1)} %reshape.180), kind=kOutput, calls=%fused_computation.3 | convolution fusion | flops 11285299200 | bytes 55918592 | tf_op jit(solution)/shard_map/qt,ftzr->fqzr/dot_general | solution.py:50
  496.6 32.2 %reshape.169 = bf16[4,168,2,32,256]{4,2,1,3,0:T(2,128)(2,1)} reshape(bf16[4,336,32,256]{3,1,2,0:T(8,128)(2,1)} %convert_bitcast_fusion) | data formatting | bytes 44040192 | tf_op jit(solution)/shard_map/reshape | solution.py:53
  528.9 22.2 %copy.66 = bf16[4,168,2,32,256]{4,2,3,0,1:T(2,128)(2,1)S(1)} copy(bf16[4,168,2,32,256]{4,2,1,3,0:T(2,128)(2,1)} %reshape.169) | data formatting | bytes 44040192 | tf_op jit(solution)/shard_map/reshape | solution.py:53
  551.0 243.3 %all_to_all.48 = bf16[4,168,2,32,256]{4,2,3,0,1:T(2,128)(2,1)} all-to-all(bf16[4,168,2,32,256]{4,2,3,0,1:T(2,128)(2,1)S(1)} %copy.66), channel_id=1, replica_groups=mesh['row'=2,'col'=16] {'row'}, dimensions={1} | all-to-all | bytes 44040192 | tf_op jit(solution)/shard_map/all_to_all | solution.py:54
  794.3 19.8 %copy.96 = bf16[4,2,84,2,32,256]{5,4,1,3,2,0:T(8,128)(2,1)} copy(bf16[4,2,84,2,32,256]{5,3,4,0,2,1:T(2,128)(2,1)} %bitcast.119) | data formatting | bytes 44040192 | tf_op jit(solution)/shard_map/all_to_all | solution.py:54
  814.1 14.9 fusion.42
  836.5 15.0 copy.72
  851.5 20.6 %copy.73 = f32[84,2,16,1024]{3,1,0,2:T(2,128)} copy(f32[84,2,16,1024]{0,3,2,1:T(8,128)} %bitcast.125) | data formatting | bytes 22020096 | tf_op jit(solution)/shard_map/reshape | solution.py:82
  886.5 15.1 fusion.21
  901.6 15.0 copy.68
  916.6 20.6 %copy.69 = f32[84,2,16,1024]{3,1,0,2:T(2,128)} copy(f32[84,2,16,1024]{0,3,2,1:T(8,128)} %bitcast.126) | data formatting | bytes 22020096 | tf_op jit(solution)/shard_map/reshape | solution.py:81
  937.3 182.1 %all-to-all-done.3 = f32[84,2,16,1024]{3,1,0,2:T(2,128)} async-done(((f32[84,2,16,1024]{3,1,0,2:T(2,128)}), f32[84,2,16,1024]{3,1,0,2:T(2,128)}, u32[]{:S(2)}, u32[]{:S(2)}) %all-to-all-start.3) | async-done | bytes 11010080 | tf_op jit(solution)/shard_map/all_to_all | solution.py:85
  1131.1 20.3 %copy.74 = f32[84,2,16,1024]{0,3,2,1:T(8,128)} copy(f32[84,2,16,1024]{3,1,0,2:T(2,128)} %all-to-all-done.3) | data formatting | bytes 22020096 | tf_op jit(solution)/shard_map/all_to_all | solution.py:85
  1151.5 24.3 %copy.76 = f32[84,2,16,16,64]{4,3,2,1,0:T(8,128)} copy(f32[84,2,16,16,64]{0,4,3,2,1:T(8,128)} %bitcast.121) | data formatting | bytes 22020096 | tf_op jit(solution)/shard_map/reshape | solution.py:88
  1175.8 186.9 %all-to-all-done.2 = f32[84,2,16,1024]{3,1,0,2:T(2,128)} async-done(((f32[84,2,16,1024]{3,1,0,2:T(2,128)}), f32[84,2,16,1024]{3,1,0,2:T(2,128)}, u32[]{:S(2)}, u32[]{:S(2)}) %all-to-all-start.2) | async-done | bytes 11010080 | tf_op jit(solution)/shard_map/all_to_all | solution.py:84
  1362.7 20.3 %copy.70 = f32[84,2,16,1024]{0,3,2,1:T(8,128)} copy(f32[84,2,16,1024]{3,1,0,2:T(2,128)} %all-to-all-done.2) | data formatting | bytes 22020096 | tf_op jit(solution)/shard_map/all_to_all | solution.py:84
  1383.0 24.3 %copy.71 = f32[84,2,16,16,64]{4,3,2,1,0:T(8,128)} copy(f32[84,2,16,16,64]{0,4,3,2,1:T(8,128)} %bitcast.122) | data formatting | bytes 22020096 | tf_op jit(solution)/shard_map/reshape | solution.py:87
  1407.3 35.9 %fusion.44 = f32[84,2,16,1024,1]{3,2,4,1,0:T(8,128)} fusion(f32[84,2,16,16,64]{4,3,2,1,0:T(8,128)} %copy.76, bf16[1024,16,64,1,1]{0,2,1,4,3:T(8,128)(2,1)} %bitcast.137), kind=kOutput, calls=%fused_computation.51 | convolution fusion | flops 33822867456 | bytes 24117248 | tf_op jit(solution)/shard_map/mpsxy,zsy->mpxz/dot_general | solution.py:94
  1443.3 21.8 %fusion.4 = f32[84,2,16,1024]{3,2,1,0:T(8,128)} fusion(f32[84,2,16,1024,1]{3,2,4,1,0:T(8,128)} %fusion.44, bf16[1024,1024]{1,0:T(8,128)(2,1)S(1)} %copy-done), kind=kOutput, calls=%fused_computation.9 | convolution fusion | flops 33822867456 | bytes 24117248 | tf_op jit(solution)/shard_map/mpxz,zk->mpxk/dot_general | solution.py:100
  1465.2 33.1 %fusion.43 = f32[84,2,16,1024,1]{3,2,4,1,0:T(8,128)} fusion(f32[84,2,16,16,64]{4,3,2,1,0:T(8,128)S(1)} %bitcast.131, bf16[16,64,1024,1,1]{2,1,0,4,3:T(8,128)(2,1)S(1)} %bitcast.114), kind=kOutput, calls=%fused_computation.50 | convolution fusion | flops 33822867456 | bytes 24117248 | tf_op jit(solution)/shard_map/mpsxy,syk->mpxk/dot_general | solution.py:93
  1498.2 40.1 %fusion.12 = f32[84,2,16,16,64]{4,3,2,1,0:T(8,128)} fusion(bf16[16,64,1024,1,1]{2,1,0,4,3:T(8,128)(2,1)S(1)} %bitcast.115, f32[84,2,16,1024]{3,2,1,0:T(8,128)} %fusion.4, f32[84,2,16,1024,1]{3,2,4,1,0:T(8,128)} %fusion.43, f32[84,16,1024]{2,1,0:T(8,128)S(1)} %bitcast.136), kind=kOutput, calls=%fused_computation.17 | convolution fusion | flops 33828372480 | bytes 40632320 | tf_op jit(solution)/shard_map/mpxk,syk->mpsxy/dot_general | solution.py:105
  1538.4 22.2 %copy.77 = f32[84,2,16,16,64]{0,4,3,2,1:T(8,128)} copy(f32[84,2,16,16,64]{4,3,2,1,0:T(8,128)} %fusion.12) | data formatting | bytes 22020096 | tf_op jit(solution)/shard_map/mpxk,syk->mpsxy/transpose | solution.py:105
  1560.6 20.6 %copy.78 = f32[84,2,16,1024]{3,1,0,2:T(2,128)} copy(f32[84,2,16,1024]{0,3,2,1:T(8,128)} %bitcast.123) | data formatting | bytes 22020096 | tf_op jit(solution)/shard_map/reshape | solution.py:106
  1586.3 14.7 copy.80
  1601.0 223.7 %all-to-all-done.4 = f32[84,2,16,1024]{3,1,0,2:T(2,128)} async-done(((f32[84,2,16,1024]{3,1,0,2:T(2,128)}), f32[84,2,16,1024]{3,1,0,2:T(2,128)}, u32[]{:S(2)}, u32[]{:S(2)}) %all-to-all-start.4) | async-done | bytes 11010080 | tf_op jit(solution)/shard_map/all_to_all | solution.py:107
  1824.7 20.3 %copy.79 = f32[84,2,16,1024]{0,3,2,1:T(8,128)} copy(f32[84,2,16,1024]{3,1,0,2:T(2,128)} %all-to-all-done.4) | data formatting | bytes 22020096 | tf_op jit(solution)/shard_map/all_to_all | solution.py:107
  1845.0 24.3 %copy.81 = f32[84,2,16,16,64]{4,3,2,1,0:T(8,128)} copy(f32[84,2,16,16,64]{0,4,3,2,1:T(8,128)} %bitcast.124) | data formatting | bytes 22020096 | tf_op jit(solution)/shard_map/reshape | solution.py:108
  1869.3 26.0 %convolution_bitcast_fusion = f32[84,2,64,256]{3,2,1,0:T(8,128)} fusion(f32[84,2,16,16,64]{4,3,2,1,0:T(8,128)} %copy.81, bf16[84,256,16,16,1]{1,3,2,4,0:T(8,128)(2,1)} %bitcast.120), kind=kOutput, calls=%fused_computation.26 | convolution fusion | flops 8455716864 | bytes 33030144 | tf_op jit(solution)/shard_map/mpsxy,mrsx->mpyr/dot_general | solution.py:112
  (52 shorter events, 79.5 us)
Async XLA Ops:
  0.0 1443.2 %copy-start = (bf16[1024,1024]{1,0:T(8,128)(2,1)S(1)}, bf16[1024,1024]{1,0:T(8,128)(2,1)}, u32[]{:S(2)}) copy-start(bf16[1024,1024]{1,0:T(8,128)(2,1)} %param.16) | copy-start | bytes 6291460
  71.9 374.6 %all-to-all-start = ((bf16[4,256,64,256]{3,1,0,2:T(8,128)(2,1)}), bf16[4,256,64,256]{3,1,0,2:T(8,128)(2,1)}, u32[]{:S(2)}, u32[]{:S(2)}) async-start(bf16[4,256,64,256]{3,1,0,2:T(8,128)(2,1)} %pad_maximum_fusion), calls=%async_computation | async-start | bytes 67108864 | tf_op jit(solution)/shard_map/all_to_all | solution.py:48
  814.1 14.9 slice-start
  814.1 15.4 slice-start.1
  814.1 16.5 slice-start.2
  872.1 9.0 copy-start.4
  872.1 247.3 %all-to-all-start.3 = ((f32[84,2,16,1024]{3,1,0,2:T(2,128)}), f32[84,2,16,1024]{3,1,0,2:T(2,128)}, u32[]{:S(2)}, u32[]{:S(2)}) async-start(f32[84,2,16,1024]{3,1,0,2:T(2,128)} %copy.73), calls=%async_computation.3 | async-start | bytes 22020096 | tf_op jit(solution)/shard_map/all_to_all | solution.py:85
  881.0 5.4 copy-start.1
  937.3 190.9 %copy-start.2 = (f32[84,256]{1,0:T(8,128)S(1)}, f32[84,256]{1,0:T(8,128)}, u32[]{:S(2)}) copy-start(f32[84,256]{1,0:T(8,128)} %param.14) | copy-start | bytes 258052
  937.3 191.0 %copy-start.3 = (f32[1024]{0:T(1024)S(1)}, f32[1024]{0:T(1024)}, u32[]{:S(2)}) copy-start(f32[1024]{0:T(1024)} %param.17) | copy-start | bytes 12292
  1119.4 243.3 %all-to-all-start.2 = ((f32[84,2,16,1024]{3,1,0,2:T(2,128)}), f32[84,2,16,1024]{3,1,0,2:T(2,128)}, u32[]{:S(2)}, u32[]{:S(2)}) async-start(f32[84,2,16,1024]{3,1,0,2:T(2,128)} %copy.69), calls=%async_computation.2 | async-start | bytes 22020096 | tf_op jit(solution)/shard_map/all_to_all | solution.py:84
  1407.3 57.8 %slice-start.3 = ((s8[22020096]{0:T(1024)(128)(4,1)}), s8[4194304]{0:T(1024)(128)(4,1)S(1)}, s32[]{:S(2)}) async-start(s8[22020096]{0:T(1024)(128)(4,1)} %bitcast.130), calls=%async_computation.8 | async-start | bytes 8388608
  1407.3 57.8 %slice-start.4 = ((s8[22020096]{0:T(1024)(128)(4,1)}), s8[4194304]{0:T(1024)(128)(4,1)S(1)}, s32[]{:S(2)}) async-start(s8[22020096]{0:T(1024)(128)(4,1)} %bitcast.130), calls=%async_computation.9 | async-start | bytes 8388608
  1407.3 57.8 %slice-start.5 = ((s8[22020096]{0:T(1024)(128)(4,1)}), s8[4194304]{0:T(1024)(128)(4,1)S(1)}, s32[]{:S(2)}) async-start(s8[22020096]{0:T(1024)(128)(4,1)} %bitcast.130), calls=%async_computation.10 | async-start | bytes 8388608
  1407.3 57.8 %slice-start.6 = ((s8[22020096]{0:T(1024)(128)(4,1)}), s8[4194304]{0:T(1024)(128)(4,1)S(1)}, s32[]{:S(2)}) async-start(s8[22020096]{0:T(1024)(128)(4,1)} %bitcast.130), calls=%async_computation.11 | async-start | bytes 8388608
  1407.3 57.8 %slice-start.7 = ((s8[22020096]{0:T(1024)(128)(4,1)}), s8[4194304]{0:T(1024)(128)(4,1)S(1)}, s32[]{:S(2)}) async-start(s8[22020096]{0:T(1024)(128)(4,1)} %bitcast.130), calls=%async_computation.12 | async-start | bytes 8388608
  1443.2 21.9 %slice-start.8 = ((s8[22020096]{0:T(1024)(128)(4,1)}), s8[1048576]{0:T(1024)(128)(4,1)S(1)}, s32[]{:S(2)}) async-start(s8[22020096]{0:T(1024)(128)(4,1)} %bitcast.130), calls=%async_computation.13 | async-start | bytes 2097152
  1443.2 55.0 %slice-start.9 = ((s8[5505024]{0:T(1024)(128)(4,1)}), s8[4194304]{0:T(1024)(128)(4,1)S(1)}, s32[]{:S(2)}) async-start(s8[5505024]{0:T(1024)(128)(4,1)} %bitcast.135), calls=%async_computation.14 | async-start | bytes 8388608
  1465.1 33.1 %slice-start.10 = ((s8[5505024]{0:T(1024)(128)(4,1)}), s8[1310720]{0:T(1024)(128)(4,1)S(1)}, s32[]{:S(2)}) async-start(s8[5505024]{0:T(1024)(128)(4,1)} %bitcast.135), calls=%async_computation.15 | async-start | bytes 2621440
  1581.1 243.6 %all-to-all-start.4 = ((f32[84,2,16,1024]{3,1,0,2:T(2,128)}), f32[84,2,16,1024]{3,1,0,2:T(2,128)}, u32[]{:S(2)}, u32[]{:S(2)}) async-start(f32[84,2,16,1024]{3,1,0,2:T(2,128)} %copy.78), calls=%async_computation.4 | async-start | bytes 22020096 | tf_op jit(solution)/shard_map/all_to_all | solution.py:107
where the time goes:
time: 1910 us; the launch traced here: 1900 us
  waiting for transfers between devices  952 us (50%)
  local copies, waits for them, and re-layouts  406 us (21%)
  blocking collectives  243 us (13%)
  matrix products  205 us (11%)
  other arithmetic  55.9 us (3%)
  starting transfers between devices  32.1 us (2%)
    all_to_all x1, waiting for transfers between devices, body(): lax.all_to_all(fields, 'row', split_axis=2, concat_axis=1, tiled=True)  359 us
    all_to_all x1, blocking collectives, body(): lax.all_to_all(spectra, 'row', split_axis=1, concat_axis=3, tiled=True)  243 us
    all_to_all x1, waiting for transfers between devices, body(): lax.all_to_all(returned, 'col', split_axis=2, concat_axis=2, tiled=True)  224 us
    all_to_all x1, waiting for transfers between devices, body(): lax.all_to_all(source_hat, 'col', split_axis=2, concat_axis=2, tiled=True)  187 us
    all_to_all x1, waiting for transfers between devices, body(): lax.all_to_all(flux_hat, 'col', split_axis=2, concat_axis=2, tiled=True)  182 us
    reshape x2, local copies, waits for them, and re-layouts, body(): spectra.reshape(4, mode_rows * row_total, 2, azimuth_rows.shape[2], radia...  54.4 us
    dot_general x1, matrix products, body(): jnp.einsum('mpxk,syk->mpsxy', coefficients, axial_blocks, precision=highest)  40.1 us
  transfers between devices with their start and end apart: 4, of which 4 were waited for; matrix products, arithmetic and copies ran while one was open for 7% of the time, Pallas kernels for 0%

commit v1 on v0

v1 whole, which is shorter than its diff:
```python
import math

import jax
import jax.numpy as jnp
from jax import lax
from jax.sharding import PartitionSpec as P

HEAT_OFFSET = 1.0
BF = jnp.bfloat16
F32 = jnp.float32


def wave_rows(first_mode, mode_count, first_angle, angle_count, circle):
    mode_ids = first_mode + jnp.arange(mode_count, dtype=jnp.int32)
    angle_ids = first_angle + jnp.arange(angle_count, dtype=jnp.int32)
    phase_index = mode_ids[:, None] * angle_ids[None, :] % circle
    angle_value = phase_index.astype(F32) * (2.0 * math.pi / circle)
    norm_factor = 1.0 / math.sqrt(circle)
    table = jnp.stack(
        [jnp.cos(angle_value) * norm_factor, -jnp.sin(angle_value) * norm_factor], axis=1
    )
    return table.astype(BF)


def chunk_count(modes):
    return max(c for c in range(1, 5) if modes % c == 0)


def body(
    velocity,
    adj_temp,
    radial_div,
    reciprocal_distance,
    radial_basis,
    radial_eig,
    axial_diff,
    axial_basis,
    axial_eig,
):
    row_total = lax.axis_size("row")
    col_total = lax.axis_size("col")
    row_place = lax.axis_index("row")
    col_place = lax.axis_index("col")
    modes = radial_basis.shape[0]
    angles, own_axial, radial_points = adj_temp.shape
    axial_points = axial_basis.shape[0]
    own_count = radial_points // col_total
    circle = angles * row_total
    parts = chunk_count(modes)
    step = modes // parts

    fluxes = (velocity.astype(F32) * adj_temp.astype(F32)[None]).astype(BF)
    heat = HEAT_OFFSET * adj_temp.astype(F32) + jnp.einsum(
        "tzj,rj->tzr", fluxes[0], radial_div, preferred_element_type=F32
    )
    fields = [heat.astype(BF), fluxes[1], fluxes[2]]

    def partial_sums(place):
        table = wave_rows(place * modes, modes, row_place * angles, angles, circle)
        heat_s, turn_s, flux_s = (
            jnp.einsum("mpt,tzr->mpzr", table, f, preferred_element_type=F32) for f in fields
        )
        mode_values = (place * modes + jnp.arange(modes, dtype=jnp.int32)).astype(F32)
        turned = jnp.stack([-turn_s[:, 1], turn_s[:, 0]], axis=1)
        source = heat_s + mode_values[:, None, None, None] * reciprocal_distance * turned
        return jnp.stack([source.astype(BF), flux_s.astype(BF)], axis=2)

    arrived = [[] for _ in range(parts)]
    for shift in range(1, row_total):
        sums = partial_sums((row_place + shift) % row_total)
        pairs = [(a, (a + shift) % row_total) for a in range(row_total)]
        for c in range(parts):
            arrived[c].append(lax.ppermute(sums[c * step : (c + 1) * step], "row", pairs))
    own = partial_sums(row_place)

    returning = jnp.einsum("zj,zk->jk", axial_diff, axial_basis, preferred_element_type=F32)
    forward = jnp.stack(
        [
            axial_basis.reshape(col_total, own_axial, axial_points),
            returning.astype(BF).reshape(col_total, own_axial, axial_points),
        ],
        axis=1,
    )
    axial_blocks = axial_basis.reshape(col_total, own_axial, axial_points)
    radial_values = lax.dynamic_slice_in_dim(radial_eig, col_place * own_count, own_count, 1)

    outs = []
    for c in range(parts):
        part = slice(c * step, (c + 1) * step)
        total = own[part].astype(F32)
        for other in arrived[c]:
            total = total + other.astype(F32)
        basis = radial_basis[part]
        hat = jnp.einsum(
            "mri,mpfzr->mipfz", basis, total.astype(BF), preferred_element_type=F32
        ).astype(BF)
        hat = hat.reshape(step, col_total, own_count, 4 * own_axial)
        hat = jnp.moveaxis(hat, 1, 0)
        lines = lax.all_to_all(hat, "col", split_axis=0, concat_axis=0, tiled=True)
        lines = lines.reshape(col_total, step, own_count, 2, 2, own_axial)
        coefficients = jnp.einsum(
            "smxpfy,sfyk->pmxk", lines, forward, preferred_element_type=F32
        )
        coefficients = coefficients / (
            radial_values[part][None, :, :, None] + axial_eig + HEAT_OFFSET
        )
        returned = jnp.einsum(
            "pmxk,syk->smxpy", coefficients.astype(BF), axial_blocks, preferred_element_type=F32
        ).astype(BF)
        returned = returned.reshape(col_total, step, own_count, 2 * own_axial)
        returned = lax.all_to_all(returned, "col", split_axis=0, concat_axis=0, tiled=True)
        returned = jnp.moveaxis(returned, 0, 1).reshape(step, radial_points, 2 * own_axial)
        outs.append(
            jnp.einsum("miw,mri->mwr", returned, basis, preferred_element_type=F32).reshape(
                step, 2, own_axial, radial_points
            )
        )
    return jnp.concatenate(outs, axis=0)


def solution(mesh):
    in_specs = (
        P(None, "row", "col", None),
        P("row", "col", None),
        P(),
        P(),
        P("row", None, None),
        P("row", None),
        P(),
        P(),
        P(),
    )
    out_specs = P("row", None, "col", None)
    return jax.shard_map(body, mesh=mesh, in_specs=in_specs, out_specs=out_specs, check_vma=False)
```

time: 1910 us -> 761 us (0.40)
  waiting for transfers between devices: 952 us -> 226 us
  blocking collectives: 243 us -> 0 us
  local copies, waits for them, and re-layouts: 406 us -> 237 us
  matrix products: 205 us -> 151 us
  starting transfers between devices: 32.1 us -> 58.2 us
  other arithmetic: 55.9 us -> 75 us
    all_to_all x4 -> x8, waiting for transfers between devices: 952 us -> 35.8 us  [the longest x4 19.5 us: body(): lines = lax.all_to_all(hat, 'col', split_axis=0, concat_axis=0, tiled=True)]
    all_to_all x1 -> x0, blocking collectives: 243 us -> none  [body(): lax.all_to_all(spectra, 'row', split_axis=1, concat_axis=3, tiled=True)]
    ppermute x0 -> x4, waiting for transfers between devices: none -> 190 us  [body(): arrived[c].append(lax.ppermute(sums[c * step:(c + 1) * step], 'row', pairs))]
    all_to_all x5 -> x0, local copies, waits for them, and re-layouts: 104 us -> none  [the longest x1 23 us: body(): lax.all_to_all(fields, 'row', split_axis=2, concat_axis=1, tiled=True)]
    reshape x8 -> x12, local copies, waits for them, and re-layouts: 189 us -> 108 us  [the longest x4 43.4 us: body(): hat = hat.reshape(step, col_total, own_count, 4 * own_axial)]
    convert_element_type x2 -> x8, local copies, waits for them, and re-layouts: 14.1 us -> 85.1 us  [the longest x4 54.8 us: body(): hat = jnp.einsum('mri,mpfzr->mipfz', basis, total.astype(BF), preferred_e...]
    dot_general x8 -> x20, matrix products: 205 us -> 151 us  [the longest x4 48.1 us: body(): jnp.einsum('pmxk,syk->smxpy', coefficients.astype(BF), axial_blocks, pref...]
    transpose x3 -> x8, local copies, waits for them, and re-layouts: 52.3 us -> 18.4 us  [the longest x4 14 us: body(): hat = jnp.moveaxis(hat, 1, 0)]
  transfers between devices with their start and end apart: 4 -> 12, of which waited for: 4 -> 6; matrix products, arithmetic and copies ran while one was open for 7% -> 43% of each run, Pallas kernels for 0% -> 0%
where the time goes in v1:
time: 761 us; the launch traced here: 747 us
  local copies, waits for them, and re-layouts  237 us (31%)
  waiting for transfers between devices  226 us (30%)
  matrix products  151 us (20%)
  other arithmetic  75 us (10%)
  starting transfers between devices  58.2 us (8%)
    ppermute x4, waiting for transfers between devices, body(): arrived[c].append(lax.ppermute(sums[c * step:(c + 1) * step], 'row', pairs))  190 us
    convert_element_type x4, local copies, waits for them, and re-layouts, body(): hat = jnp.einsum('mri,mpfzr->mipfz', basis, total.astype(BF), preferred_e...  54.8 us
    dot_general x4, matrix products, body(): jnp.einsum('pmxk,syk->smxpy', coefficients.astype(BF), axial_blocks, pref...  48.1 us
    reshape x4, local copies, waits for them, and re-layouts, body(): hat = hat.reshape(step, col_total, own_count, 4 * own_axial)  43.4 us
    dot_general x6, matrix products, partial_sums(): jnp.einsum('mpt,tzr->mpzr', table, f, preferred_element_type=F32)  42.5 us
    reshape x4, local copies, waits for them, and re-layouts, body(): lines = lines.reshape(col_total, step, own_count, 2, 2, own_axial)  41.6 us
    convert_element_type x4, local copies, waits for them, and re-layouts, body(): returned = jnp.einsum('pmxk,syk->smxpy', coefficients.astype(BF), axial_b...  30.2 us
    all_to_all x4, starting transfers between devices, body(): lines = lax.all_to_all(hat, 'col', split_axis=0, concat_axis=0, tiled=True)  29 us
  transfers between devices with their start and end apart: 12, of which 6 were waited for; matrix products, arithmetic and copies ran while one was open for 43% of the time, Pallas kernels for 0%

profile of v1, /device:TPU:11, one launch (start us, length us, event | category | flops | bytes accessed | tf_op | source)
XLA Modules:
  0.0 747.2 jit_solution(15317897533672225099)
XLA Ops:
  0.0 14.1 %copy_convert_fusion.1 = f32[256,64,256]{2,0,1:T(8,128)} fusion(bf16[256,64,256]{2,1,0:T(8,128)(2,1)} %param.10), kind=kLoop, calls=%fused_computation.29 | loop fusion | flops 4194304 | bytes 25165824 | tf_op jit(solution)/shard_map/convert_element_type | solution.py:53
  14.2 23.8 %multiply_convert_fusion = bf16[3,256,64,256]{3,1,2,0:T(8,128)(2,1)} fusion(bf16[3,256,64,256]{3,2,1,0:T(8,128)(2,1)} %param.9, f32[256,64,256]{2,0,1:T(8,128)} %copy_convert_fusion.1), kind=kLoop, calls=%fused_computation | loop fusion | flops 37748736 | bytes 67108864 | tf_op jit(solution)/shard_map/convert_element_type | solution.py:52
  38.8 9.3 %fusion.8 = f32[84,2,64,256]{3,0,2,1:T(8,128)} fusion(bf16[3,256,64,256]{3,1,2,0:T(8,128)(2,1)} %multiply_convert_fusion, bf16[84,1,256]{2,0,1:T(8,128)(2,1)S(1)} %get-tuple-element.27, bf16[84,1,256]{2,0,1:T(8,128)(2,1)S(1)} %get-tuple-element.28), kind=kOutput, calls=%fused_computation.30 | convolution fusion | flops 1409458176 | bytes 19484672 | tf_op jit(solution)/shard_map/mpt,tzr->mpzr/dot_general | solution.py:61
  53.2 19.3 %add_convert_fusion = bf16[256,64,256]{2,0,1:T(8,128)(2,1)} fusion(bf16[3,256,64,256]{3,1,2,0:T(8,128)(2,1)} %multiply_convert_fusion, bf16[256,64,256]{2,1,0:T(8,128)(2,1)} %param.10, bf16[256,256]{1,0:T(8,128)(2,1)S(1)} %copy-done.12), kind=kOutput, calls=%fused_computation.1 | convolution fusion | flops 2160066560 | bytes 25296896 | tf_op jit(solution)/shard_map/tzj,rj->tzr/dot_general | solution.py:53
  72.5 9.6 %slice_negate_fusion = (f32[84,1,64,256]{3,0,2,1:T(8,128)}, f32[84,1,64,256]{3,0,2,1:T(8,128)}) fusion(f32[84,2,64,256]{3,0,2,1:T(8,128)} %fusion.8), kind=kLoop, calls=%fused_computation.35 | loop fusion | flops 1376256 | bytes 22020096 | tf_op jit(solution)/shard_map/neg | solution.py:64
  82.1 8.5 %fusion.12 = bf16[84,2,1,64,256]{4,0,3,1,2:T(8,128)(2,1)S(1)} fusion(f32[84,1,64,256]{3,0,2,1:T(8,128)} %get-tuple-element.12, f32[84,1,64,256]{3,0,2,1:T(8,128)} %get-tuple-element.11, f32[84,256]{1,0:T(8,128)S(1)} %get-tuple-element.26, bf16[256,64,256]{2,0,1:T(8,128)(2,1)} %add_convert_fusion, bf16[84,1,256]{2,0,1:T(8,128)(2,1)S(1)} %get-tuple-element.27, ...), kind=kOutput, calls=%fused_computation.34 | convolution fusion | flops 1420468224 | bytes 25075712 | tf_op jit(solution)/shard_map/mpt,tzr->mpzr/dot_general | solution.py:61
  100.8 9.3 %fusion.9 = f32[84,2,64,256]{3,0,2,1:T(8,128)} fusion(bf16[3,256,64,256]{3,1,2,0:T(8,128)(2,1)} %multiply_convert_fusion, bf16[84,1,256]{2,0,1:T(8,128)(2,1)S(1)} %get-tuple-element.22, bf16[84,1,256]{2,0,1:T(8,128)(2,1)S(1)} %get-tuple-element.21), kind=kOutput, calls=%fused_computation.31 | convolution fusion | flops 1409458176 | bytes 19484672 | tf_op jit(solution)/shard_map/mpt,tzr->mpzr/dot_general | solution.py:61
  140.6 8.7 %fusion.14 = bf16[84,2,1,64,256]{4,3,2,1,0:T(8,128)(2,1)S(1)} fusion(f32[84,1,64,256]{3,2,1,0:T(8,128)S(1)} %bitcast.220, f32[84,1,64,256]{3,2,1,0:T(8,128)} %copy_negate_fusion, f32[84,2,64,256]{3,0,2,1:T(8,128)S(1)} %fusion.6, f32[84,256]{1,0:T(8,128)S(1)} %get-tuple-element.25), kind=kLoop, calls=%fused_computation.38 | loop fusion | flops 11010048 | bytes 27611136 | tf_op jit(solution)/shard_map/stack | solution.py:66
  149.3 11.2 %collective-permute-done = bf16[21,2,2,64,256]{4,3,2,1,0:T(8,128)(2,1)} collective-permute-done((bf16[21,2,2,64,256]{4,3,2,1,0:T(8,128)(2,1)}, bf16[21,2,2,64,256]{4,3,2,1,0:T(8,128)(2,1)}, u32[]{:S(2)}, u32[]{:S(2)}) %collective-permute-start) | collective-permute-done | bytes 2752544 | tf_op jit(solution)/shard_map/ppermute | solution.py:73
  165.7 13.7 %copy.117 = bf16[21,256,2,2,64]{4,3,2,1,0:T(2,128)(2,1)} copy(bf16[21,256,2,2,64]{1,4,3,2,0:T(8,128)(2,1)} %convert_bitcast_fusion.8) | data formatting | bytes 5505024 | tf_op jit(solution)/shard_map/convert_element_type | solution.py:96
  179.4 10.8 %reshape.429 = bf16[21,16,16,256]{3,2,1,0:T(8,128)(2,1)} reshape(bf16[21,256,2,2,64]{4,3,2,1,0:T(2,128)(2,1)} %copy.117) | data formatting | bytes 5505024 | tf_op jit(solution)/shard_map/reshape | solution.py:97
  205.0 59.6 %collective-permute-done.1 = bf16[21,2,2,64,256]{4,3,2,1,0:T(8,128)(2,1)S(1)} collective-permute-done((bf16[21,2,2,64,256]{4,3,2,1,0:T(8,128)(2,1)S(1)}, bf16[21,2,2,64,256]{4,3,2,1,0:T(8,128)(2,1)S(1)}, u32[]{:S(2)}, u32[]{:S(2)}) %collective-permute-start.1) | collective-permute-done | bytes 2752544 | tf_op jit(solution)/shard_map/ppermute | solution.py:73
  269.7 13.7 %copy.124 = bf16[21,256,2,2,64]{4,3,2,1,0:T(2,128)(2,1)} copy(bf16[21,256,2,2,64]{1,4,3,2,0:T(8,128)(2,1)} %convert_bitcast_fusion.6) | data formatting | bytes 5505024 | tf_op jit(solution)/shard_map/convert_element_type | solution.py:96
  283.4 10.9 %reshape.435 = bf16[21,16,16,256]{3,2,1,0:T(8,128)(2,1)} reshape(bf16[21,256,2,2,64]{4,3,2,1,0:T(2,128)(2,1)} %copy.124) | data formatting | bytes 5505024 | tf_op jit(solution)/shard_map/reshape | solution.py:97
  309.1 59.6 %collective-permute-done.2 = bf16[21,2,2,64,256]{4,3,2,1,0:T(8,128)(2,1)S(1)} collective-permute-done((bf16[21,2,2,64,256]{4,3,2,1,0:T(8,128)(2,1)S(1)}, bf16[21,2,2,64,256]{4,3,2,1,0:T(8,128)(2,1)S(1)}, u32[]{:S(2)}, u32[]{:S(2)}) %collective-permute-start.2) | collective-permute-done | bytes 2752544 | tf_op jit(solution)/shard_map/ppermute | solution.py:73
  373.8 13.7 %copy.131 = bf16[21,256,2,2,64]{4,3,2,1,0:T(2,128)(2,1)} copy(bf16[21,256,2,2,64]{1,4,3,2,0:T(8,128)(2,1)} %convert_bitcast_fusion.4) | data formatting | bytes 5505024 | tf_op jit(solution)/shard_map/convert_element_type | solution.py:96
  387.5 10.9 %reshape.440 = bf16[21,16,16,256]{3,2,1,0:T(8,128)(2,1)} reshape(bf16[21,256,2,2,64]{4,3,2,1,0:T(2,128)(2,1)} %copy.131) | data formatting | bytes 5505024 | tf_op jit(solution)/shard_map/reshape | solution.py:97
  412.7 59.6 %collective-permute-done.3 = bf16[21,2,2,64,256]{4,3,2,1,0:T(8,128)(2,1)S(1)} collective-permute-done((bf16[21,2,2,64,256]{4,3,2,1,0:T(8,128)(2,1)S(1)}, bf16[21,2,2,64,256]{4,3,2,1,0:T(8,128)(2,1)S(1)}, u32[]{:S(2)}, u32[]{:S(2)}) %collective-permute-start.3) | collective-permute-done | bytes 2752544 | tf_op jit(solution)/shard_map/ppermute | solution.py:73
  477.4 13.7 %copy.138 = bf16[21,256,2,2,64]{4,3,2,1,0:T(2,128)(2,1)} copy(bf16[21,256,2,2,64]{1,4,3,2,0:T(8,128)(2,1)} %convert_bitcast_fusion.2) | data formatting | bytes 5505024 | tf_op jit(solution)/shard_map/convert_element_type | solution.py:96
  491.1 10.9 %reshape.445 = bf16[21,16,16,256]{3,2,1,0:T(8,128)(2,1)} reshape(bf16[21,256,2,2,64]{4,3,2,1,0:T(2,128)(2,1)} %copy.138) | data formatting | bytes 5505024 | tf_op jit(solution)/shard_map/reshape | solution.py:97
  519.1 10.5 %reshape.430 = bf16[16,21,16,2,2,64]{5,4,3,2,1,0:T(2,128)(2,1)} reshape(bf16[16,21,16,256]{3,2,1,0:T(8,128)(2,1)} %all-to-all-done) | data formatting | bytes 5505024 | tf_op jit(solution)/shard_map/reshape | solution.py:100
  529.5 11.8 %convert_bitcast_fusion.7 = bf16[16,21,16,2,64]{4,2,0,1,3:T(8,128)(2,1)} fusion(bf16[16,64,1024,1,1]{2,1,0,4,3:T(8,128)(2,1)} %bitcast.235, bf16[16,21,16,2,2,64]{5,4,3,2,1,0:T(2,128)(2,1)} %reshape.430, f32[21,16,1024]{2,1,0:T(8,128)S(1)} %copy-done.7, bf16[16,1,64,1024]{3,2,0,1:T(8,128)(2,1)} %bitcast.243, bf16[16,1,64,1024]{3,2,0,1:T(8,128)(2,1)} %bitcast.236), kind=kOutput, calls=%fused_computation.84 | convolution fusion | flops 4238311424 | bytes 11796480 | tf_op jit(solution)/shard_map/pmxk,syk->smxpy/dot_general | solution.py:107
  541.4 7.6 %copy.120 = bf16[16,21,16,2,64]{4,3,2,1,0:T(2,128)(2,1)} copy(bf16[16,21,16,2,64]{4,2,0,1,3:T(8,128)(2,1)} %convert_bitcast_fusion.7) | data formatting | bytes 2752512 | tf_op jit(solution)/shard_map/convert_element_type | solution.py:109
  554.7 19.5 %all-to-all-done.6 = bf16[16,21,16,256]{3,2,1,0:T(8,128)(2,1)} async-done(((bf16[16,21,16,256]{3,2,1,0:T(8,128)(2,1)}), bf16[16,21,16,256]{3,2,1,0:T(8,128)(2,1)}, u32[]{:S(2)}, u32[]{:S(2)}) %all-to-all-start.6) | async-done | bytes 2752544 | tf_op jit(solution)/shard_map/all_to_all | solution.py:99
  579.0 10.4 %reshape.436 = bf16[16,21,16,2,2,64]{5,4,3,2,1,0:T(2,128)(2,1)} reshape(bf16[16,21,16,256]{3,2,1,0:T(8,128)(2,1)} %all-to-all-done.2) | data formatting | bytes 5505024 | tf_op jit(solution)/shard_map/reshape | solution.py:100
  589.4 11.8 %convert_bitcast_fusion.5 = bf16[16,21,16,2,64]{4,2,0,1,3:T(8,128)(2,1)} fusion(bf16[16,64,1024,1,1]{2,1,0,4,3:T(8,128)(2,1)} %bitcast.237, bf16[16,21,16,2,2,64]{5,4,3,2,1,0:T(2,128)(2,1)} %reshape.436, f32[21,16,1024]{2,1,0:T(8,128)S(1)} %get-tuple-element.18, bf16[16,1,64,1024]{3,2,0,1:T(8,128)(2,1)} %bitcast.244, bf16[16,1,64,1024]{3,2,0,1:T(8,128)(2,1)} %bitcast.238), kind=kOutput, calls=%fused_computation.82 | convolution fusion | flops 4238311424 | bytes 11796480 | tf_op jit(solution)/shard_map/pmxk,syk->smxpy/dot_general | solution.py:107
  620.8 10.4 %reshape.441 = bf16[16,21,16,2,2,64]{5,4,3,2,1,0:T(2,128)(2,1)} reshape(bf16[16,21,16,256]{3,2,1,0:T(8,128)(2,1)} %all-to-all-done.4) | data formatting | bytes 5505024 | tf_op jit(solution)/shard_map/reshape | solution.py:100
  631.2 12.3 %convert_bitcast_fusion.3 = bf16[16,21,16,2,64]{4,2,0,1,3:T(8,128)(2,1)} fusion(bf16[16,64,1024,1,1]{2,1,0,4,3:T(8,128)(2,1)} %bitcast.239, bf16[16,21,16,2,2,64]{5,4,3,2,1,0:T(2,128)(2,1)} %reshape.441, f32[21,16,1024]{2,1,0:T(8,128)} %get-tuple-element.19, bf16[16,1,64,1024]{3,2,0,1:T(8,128)(2,1)} %bitcast.245, bf16[16,1,64,1024]{3,2,0,1:T(8,128)(2,1)} %bitcast.240), kind=kOutput, calls=%fused_computation.80 | convolution fusion | flops 4238311424 | bytes 11796480 | tf_op jit(solution)/shard_map/pmxk,syk->smxpy/dot_general | solution.py:107
  643.5 7.6 %copy.134 = bf16[16,21,16,2,64]{4,3,2,1,0:T(2,128)(2,1)} copy(bf16[16,21,16,2,64]{4,2,0,1,3:T(8,128)(2,1)} %convert_bitcast_fusion.3) | data formatting | bytes 2752512 | tf_op jit(solution)/shard_map/convert_element_type | solution.py:109
  663.0 10.4 %reshape.446 = bf16[16,21,16,2,2,64]{5,4,3,2,1,0:T(2,128)(2,1)} reshape(bf16[16,21,16,256]{3,2,1,0:T(8,128)(2,1)} %all-to-all-done.6) | data formatting | bytes 5505024 | tf_op jit(solution)/shard_map/reshape | solution.py:100
  673.4 12.2 %convert_bitcast_fusion.1 = bf16[16,21,16,2,64]{4,2,0,1,3:T(8,128)(2,1)} fusion(bf16[16,64,1024,1,1]{2,1,0,4,3:T(8,128)(2,1)} %bitcast.241, bf16[16,21,16,2,2,64]{5,4,3,2,1,0:T(2,128)(2,1)} %reshape.446, f32[21,16,1024]{2,1,0:T(8,128)} %get-tuple-element.20, bf16[16,1,64,1024]{3,2,0,1:T(8,128)(2,1)} %bitcast.246, bf16[16,1,64,1024]{3,2,0,1:T(8,128)(2,1)} %bitcast.242), kind=kOutput, calls=%fused_computation.78 | convolution fusion | flops 4238311424 | bytes 11796480 | tf_op jit(solution)/shard_map/pmxk,syk->smxpy/dot_general | solution.py:107
  720.7 16.3 %all-to-all-done.7 = bf16[16,21,16,128]{3,2,1,0:T(8,128)(2,1)} async-done(((bf16[16,21,16,128]{3,2,1,0:T(8,128)(2,1)}), bf16[16,21,16,128]{3,2,1,0:T(8,128)(2,1)}, u32[]{:S(2)}, u32[]{:S(2)}) %all-to-all-start.7) | async-done | bytes 1376288 | tf_op jit(solution)/shard_map/all_to_all | solution.py:111
  (92 shorter events, 215.3 us)
Async XLA Ops:
  0.0 515.3 %copy-start = (bf16[1024,1024]{1,0:T(8,128)(2,1)S(1)}, bf16[1024,1024]{1,0:T(8,128)(2,1)}, u32[]{:S(2)}) copy-start(bf16[1024,1024]{1,0:T(8,128)(2,1)} %param.15) | copy-start | bytes 6291460
  48.1 5.1 copy-start.12
  72.5 9.6 %copy-start.10 = (f32[256]{0:T(256)S(1)}, f32[256]{0:T(256)}, u32[]{:S(2)}) copy-start(f32[256]{0:T(256)} %param.12) | copy-start | bytes 3076
  99.6 60.9 %collective-permute-start = (bf16[21,2,2,64,256]{4,3,2,1,0:T(8,128)(2,1)}, bf16[21,2,2,64,256]{4,3,2,1,0:T(8,128)(2,1)}, u32[]{:S(2)}, u32[]{:S(2)}) collective-permute-start(bf16[21,2,2,64,256]{4,3,2,1,0:T(8,128)(2,1)} %copy.116), channel_id=1, source_target_pairs={{0,16},{16,0},{1,17},{17,1},{2,18},{18,2},{3,19},{19,3},{4,20},{20... | collective-permute-start | bytes 8257544 | tf_op jit(solution)/shard_map/ppermute | solution.py:73
  130.9 29.5 %copy-start.3 = (bf16[84,2,64,256]{3,2,1,0:T(8,128)(2,1)}, bf16[84,2,64,256]{3,2,1,0:T(8,128)(2,1)S(1)}, u32[]{:S(2)}) copy-start(bf16[84,2,64,256]{3,2,1,0:T(8,128)(2,1)S(1)} %copy.208) | copy-start | bytes 16515076
  130.9 9.6 %slice-start = ((s8[5505024]{0:T(1024)(128)(4,1)}), s8[1310720]{0:T(1024)(128)(4,1)S(1)}, s32[]{:S(2)}) async-start(s8[5505024]{0:T(1024)(128)(4,1)} %bitcast.219), calls=%async_computation.8 | async-start | bytes 2621440
  135.3 5.2 slice-start.1
  149.3 11.2 %copy-start.2 = (bf16[84,2,1,64,256]{4,3,2,1,0:T(8,128)(2,1)}, bf16[84,2,1,64,256]{4,3,2,1,0:T(8,128)(2,1)S(1)}, u32[]{:S(2)}) copy-start(bf16[84,2,1,64,256]{4,3,2,1,0:T(8,128)(2,1)S(1)} %fusion.14) | copy-start | bytes 16515076
  193.7 104.1 %all-to-all-start = ((bf16[16,21,16,256]{3,2,1,0:T(8,128)(2,1)}), bf16[16,21,16,256]{3,2,1,0:T(8,128)(2,1)}, u32[]{:S(2)}, u32[]{:S(2)}) async-start(bf16[16,21,16,256]{3,2,1,0:T(8,128)(2,1)} %copy.118), calls=%async_computation | async-start | bytes 5505024 | tf_op jit(solution)/shard_map/all_to_all | solution.py:99
  203.7 60.9 %collective-permute-start.1 = (bf16[21,2,2,64,256]{4,3,2,1,0:T(8,128)(2,1)S(1)}, bf16[21,2,2,64,256]{4,3,2,1,0:T(8,128)(2,1)S(1)}, u32[]{:S(2)}, u32[]{:S(2)}) collective-permute-start(bf16[21,2,2,64,256]{4,3,2,1,0:T(8,128)(2,1)S(1)} %copy.123), channel_id=1, source_target_pairs={{0,16},{16,0},{1,17},{17,1},{2,18},{18,2},{3,19},{19,3},{4,20},{20... | collective-permute-start | bytes 8257544 | tf_op jit(solution)/shard_map/ppermute | solution.py:73
  297.8 104.1 %all-to-all-start.2 = ((bf16[16,21,16,256]{3,2,1,0:T(8,128)(2,1)}), bf16[16,21,16,256]{3,2,1,0:T(8,128)(2,1)}, u32[]{:S(2)}, u32[]{:S(2)}) async-start(bf16[16,21,16,256]{3,2,1,0:T(8,128)(2,1)} %copy.125), calls=%async_computation.2 | async-start | bytes 5505024 | tf_op jit(solution)/shard_map/all_to_all | solution.py:99
  307.8 60.9 %collective-permute-start.2 = (bf16[21,2,2,64,256]{4,3,2,1,0:T(8,128)(2,1)S(1)}, bf16[21,2,2,64,256]{4,3,2,1,0:T(8,128)(2,1)S(1)}, u32[]{:S(2)}, u32[]{:S(2)}) collective-permute-start(bf16[21,2,2,64,256]{4,3,2,1,0:T(8,128)(2,1)S(1)} %copy.130), channel_id=1, source_target_pairs={{0,16},{16,0},{1,17},{17,1},{2,18},{18,2},{3,19},{19,3},{4,20},{20... | collective-permute-start | bytes 8257544 | tf_op jit(solution)/shard_map/ppermute | solution.py:73
  401.9 103.6 %all-to-all-start.4 = ((bf16[16,21,16,256]{3,2,1,0:T(8,128)(2,1)}), bf16[16,21,16,256]{3,2,1,0:T(8,128)(2,1)}, u32[]{:S(2)}, u32[]{:S(2)}) async-start(bf16[16,21,16,256]{3,2,1,0:T(8,128)(2,1)} %copy.132), calls=%async_computation.4 | async-start | bytes 5505024 | tf_op jit(solution)/shard_map/all_to_all | solution.py:99
  411.3 60.9 %collective-permute-start.3 = (bf16[21,2,2,64,256]{4,3,2,1,0:T(8,128)(2,1)S(1)}, bf16[21,2,2,64,256]{4,3,2,1,0:T(8,128)(2,1)S(1)}, u32[]{:S(2)}, u32[]{:S(2)}) collective-permute-start(bf16[21,2,2,64,256]{4,3,2,1,0:T(8,128)(2,1)S(1)} %copy.137), channel_id=1, source_target_pairs={{0,16},{16,0},{1,17},{17,1},{2,18},{18,2},{3,19},{19,3},{4,20},{20... | collective-permute-start | bytes 8257544 | tf_op jit(solution)/shard_map/ppermute | solution.py:73
  501.9 10.9 %copy-start.8 = (f32[84,256]{1,0:T(8,128)S(1)}, f32[84,256]{1,0:T(8,128)}, u32[]{:S(2)}) copy-start(f32[84,256]{1,0:T(8,128)} %param.14) | copy-start | bytes 258052
  505.5 7.5 copy-start.9
  505.5 68.8 %all-to-all-start.6 = ((bf16[16,21,16,256]{3,2,1,0:T(8,128)(2,1)}), bf16[16,21,16,256]{3,2,1,0:T(8,128)(2,1)}, u32[]{:S(2)}, u32[]{:S(2)}) async-start(bf16[16,21,16,256]{3,2,1,0:T(8,128)(2,1)} %copy.139), calls=%async_computation.6 | async-start | bytes 5505024 | tf_op jit(solution)/shard_map/all_to_all | solution.py:99
  512.8 2.5 copy-start.11
  519.0 10.5 %copy-start.7 = (f32[21,16,1024]{2,1,0:T(8,128)S(1)}, f32[21,16,1024]{2,1,0:T(8,128)}, u32[]{:S(2)}) copy-start(f32[21,16,1024]{2,1,0:T(8,128)} %get-tuple-element.17) | copy-start | bytes 4128772
  574.2 40.1 %all-to-all-start.1 = ((bf16[16,21,16,128]{3,2,1,0:T(8,128)(2,1)}), bf16[16,21,16,128]{3,2,1,0:T(8,128)(2,1)S(1)}, u32[]{:S(2)}, u32[]{:S(2)}) async-start(bf16[16,21,16,128]{3,2,1,0:T(8,128)(2,1)} %reshape.432), calls=%async_computation.1 | async-start | bytes 2752512 | tf_op jit(solution)/shard_map/all_to_all | solution.py:111
  614.3 42.3 %all-to-all-start.3 = ((bf16[16,21,16,128]{3,2,1,0:T(8,128)(2,1)}), bf16[16,21,16,128]{3,2,1,0:T(8,128)(2,1)S(1)}, u32[]{:S(2)}, u32[]{:S(2)}) async-start(bf16[16,21,16,128]{3,2,1,0:T(8,128)(2,1)} %reshape.437), calls=%async_computation.3 | async-start | bytes 2752512 | tf_op jit(solution)/shard_map/all_to_all | solution.py:111
  656.6 42.1 %all-to-all-start.5 = ((bf16[16,21,16,128]{3,2,1,0:T(8,128)(2,1)}), bf16[16,21,16,128]{3,2,1,0:T(8,128)(2,1)}, u32[]{:S(2)}, u32[]{:S(2)}) async-start(bf16[16,21,16,128]{3,2,1,0:T(8,128)(2,1)} %reshape.442), calls=%async_computation.5 | async-start | bytes 2752512 | tf_op jit(solution)/shard_map/all_to_all | solution.py:111
  698.7 38.3 %all-to-all-start.7 = ((bf16[16,21,16,128]{3,2,1,0:T(8,128)(2,1)}), bf16[16,21,16,128]{3,2,1,0:T(8,128)(2,1)}, u32[]{:S(2)}, u32[]{:S(2)}) async-start(bf16[16,21,16,128]{3,2,1,0:T(8,128)(2,1)} %reshape.447), calls=%async_computation.7 | async-start | bytes 2752512 | tf_op jit(solution)/shard_map/all_to_all | solution.py:111
  737.0 5.5 copy-start.4
  737.0 5.5 copy-start.5
  737.0 5.5 copy-start.6
  742.5 4.4 copy-start.1
